TPU v7x, 256 devices: a whole 4x4x8 slice. The times are simulated.
256 devices in a mesh: dp: 8 (over x, y_hi), mp: 32 (over z, y_lo, core).
Axes of the slice: x: 4, y: 4 (y_hi: 2, y_lo: 2; y = y_hi * 2 + y_lo), z: 8, core: 2. Of those that a mesh axis runs over, the one named last changes fastest.
Arguments:
- hidden: bfloat16 [64, 128, 18432], P('dp', None, 'mp'), may hold values from -400 to 400
- cotangent: bfloat16 [64, 128, 4608], P('dp', 'mp'), may hold values from -8 to 8
- w_down: bfloat16 [18432, 4608], P('mp', 'dp'), may hold values from -0.046875 to 0.046875
- lengths: int32 [64], P('dp'), may hold values from 1 to 128, 6144 in all
Outputs:
- weight_grad: float32 [18432, 4608], P('mp', 'dp')
- d_hidden: bfloat16 [64, 128, 18432], P('dp', None, 'mp')
All inputs are finite; a program needn't handle non-finite values. No bound on the sum of `lengths` on one device may be relied on, other than what follows from the above.
Results may differ from a plain program's by a relative error of at most 0.003.
Values may be sent and summed in bfloat16 or wider, within the bound.
No kernel may reach another device: no remote copies, remote signals or barrier semaphores. Data moves between devices by JAX's collectives and lax.ppermute only.
A program may use at most 256 MiB of HBM per device.

v0:
```python
import math
import jax
import jax.numpy as jnp
from jax import lax
from jax.sharding import PartitionSpec as P


def body(hidden, cotangent, w_down, lengths):
    seqs = hidden.shape[0]
    whole = lax.all_gather(cotangent, "mp", axis=1, tiled=True)
    seq_len = whole.shape[1]
    width = whole.shape[2]
    positions = jnp.arange(seq_len, dtype=jnp.int32)
    keep = positions[None, :] < lengths[:, None]
    masked = jnp.where(keep[:, :, None], whole, jnp.zeros((), whole.dtype))
    flat = masked.reshape(seqs * seq_len, width)
    units = hidden.shape[2]
    part = flat
    grads_in = lax.dot_general(
        part,
        lax.all_gather(w_down, "dp", axis=1, tiled=True),
        (((1,), (1,)), ((), ())),
        preferred_element_type=jnp.float32,
    )
    d_hidden = grads_in.astype(jnp.bfloat16).reshape(seqs, seq_len, units)
    cot_gram = jnp.einsum("bsd,btd->bst", masked, masked, preferred_element_type=jnp.float32)
    hid_gram = jnp.einsum("bsf,btf->bst", hidden, hidden, preferred_element_type=jnp.float32)
    summed = lax.psum(hid_gram.astype(jnp.bfloat16), "mp").astype(jnp.float32)
    sq_norm = jnp.sum(summed * cot_gram, axis=(1, 2))
    full_units = units * lax.axis_size("mp")
    groups = lax.axis_size("dp")
    radius = math.sqrt(full_units * width / (seqs * groups))
    clip_scale = radius / jnp.sqrt(sq_norm + 1e-06)
    share = width // groups
    running = jnp.zeros((share * lax.axis_size("dp"), units), jnp.float32)
    for which in range(seqs):
        part = masked[which]
        running = running + clip_scale[which] * lax.dot_general(
            part, hidden[which], (((0,), (0,)), ((), ())), preferred_element_type=jnp.float32
        )
    local = lax.psum_scatter(running, "dp", scatter_dimension=0, tiled=True)
    weight_grad = local.T
    return (weight_grad, d_hidden)


def solution(mesh):
    in_specs = (P("dp", None, "mp"), P("dp", "mp", None), P("mp", "dp"), P("dp"))
    out_specs = (P("mp", "dp"), P("dp", None, "mp"))
    return jax.shard_map(body, mesh=mesh, in_specs=in_specs, out_specs=out_specs, check_vma=False)
```

profile of v0, /device:TPU:1, one launch (start us, length us, event | category | flops | bytes accessed | tf_op | source)
XLA Modules:
  0.0 570.3 jit_solution(3020541415049871727)
XLA Ops:
  7.2 1.7 copy.14
  9.0 0.0 all-reduce.2.cloned.1.call-start
  9.0 3.0 convolution_convert_fusion.1
  12.1 2.3 copy.16
  14.4 0.0 reduce-scatter.2.cloned.1.call-start
  14.4 0.7 iota_compare_fusion
  15.1 71.8 %all-gather.3.cloned.1.call-done = bf16[8,128,4608]{2,0,1:T(8,128)(2,1)} async-done(((bf16[8,4,4608]{2,0,1:T(8,128)(2,1)}), bf16[8,128,4608]{2,0,1:T(8,128)(2,1)}) %all-gather.3.cloned.1.call-update) | async-done | bytes 9437200 | tf_op jit(solution)/shard_map/all_gather | solution.py:10
  86.9 13.3 %copy_select_fusion = bf16[8,128,4608]{2,1,0:T(8,128)(2,1)} fusion(bf16[8,128,4608]{2,0,1:T(8,128)(2,1)} %all-gather.3.cloned.1.call-done, pred[8,128]{1,0:T(8,128)(4,1)S(1)} %iota_compare_fusion), kind=kLoop, calls=%fused_computation.1 | loop fusion | flops 4718592 | bytes 18875392 | tf_op jit(solution)/shard_map/jit(_where)/select_n | solution.py:15
  100.2 215.5 %all-reduce.2.cloned.1.call-done = bf16[8,128,128]{2,1,0:T(8,128)(2,1)} async-done(((bf16[8,128,128]{2,1,0:T(8,128)(2,1)}), bf16[8,128,128]{2,1,0:T(8,128)(2,1)}) %all-reduce.2.cloned.1.call-update) | async-done | bytes 262160 | tf_op jit(solution)/shard_map/psum | solution.py:28
  315.7 9.1 %fusion.8 = f32[8]{0:T(128)S(1)} fusion(bf16[8,128,4608]{2,1,0:T(8,128)(2,1)} %copy_select_fusion, bf16[8,128,128]{2,1,0:T(8,128)(2,1)} %all-reduce.2.cloned.1.call-done), kind=kOutput, calls=%fused_computation.22 | convolution fusion | flops 1208352768 | bytes 9699360 | tf_op jit(solution)/shard_map/bsd,btd->bst/dot_general | solution.py:26
  324.7 0.7 fusion.25
  325.4 7.9 %fusion.1 = f32[4608,576]{1,0:T(8,128)} fusion(bf16[8,128,4608]{2,1,0:T(8,128)(2,1)} %copy_select_fusion, bf16[8,128,576]{1,2,0:T(8,128)(2,1)S(1)} %copy-done), kind=kOutput, calls=%fused_computation.9 | convolution fusion | flops 679477248 | bytes 11943936 | tf_op jit(solution)/shard_map/dot_general | solution.py:38
  333.4 6.1 %fusion.2 = f32[4608,576]{1,0:T(8,128)} fusion(bf16[8,128,4608]{2,1,0:T(8,128)(2,1)S(1)} %bitcast.71, bf16[8,128,576]{1,2,0:T(8,128)(2,1)S(1)} %copy-done), kind=kOutput, calls=%fused_computation.11 | convolution fusion | flops 679477248 | bytes 11943936 | tf_op jit(solution)/shard_map/dot_general | solution.py:38
  339.5 6.2 %fusion.3 = f32[4608,576]{1,0:T(8,128)} fusion(bf16[8,128,4608]{2,1,0:T(8,128)(2,1)S(1)} %bitcast.71, bf16[8,128,576]{1,2,0:T(8,128)(2,1)S(1)} %copy-done), kind=kOutput, calls=%fused_computation.13 | convolution fusion | flops 679477248 | bytes 11943936 | tf_op jit(solution)/shard_map/dot_general | solution.py:38
  345.7 6.0 %fusion.4 = f32[4608,576]{1,0:T(8,128)} fusion(bf16[8,128,4608]{2,1,0:T(8,128)(2,1)S(1)} %bitcast.71, bf16[8,128,576]{1,2,0:T(8,128)(2,1)S(1)} %copy-done), kind=kOutput, calls=%fused_computation.15 | convolution fusion | flops 679477248 | bytes 11943936 | tf_op jit(solution)/shard_map/dot_general | solution.py:38
  351.7 6.1 %fusion.5 = f32[4608,576]{1,0:T(8,128)} fusion(bf16[8,128,4608]{2,1,0:T(8,128)(2,1)S(1)} %bitcast.71, bf16[8,128,576]{1,2,0:T(8,128)(2,1)S(1)} %copy-done), kind=kOutput, calls=%fused_computation.17 | convolution fusion | flops 679477248 | bytes 11943936 | tf_op jit(solution)/shard_map/dot_general | solution.py:38
  357.7 6.4 %fusion.6 = f32[4608,576]{1,0:T(8,128)} fusion(bf16[8,128,4608]{2,1,0:T(8,128)(2,1)S(1)} %bitcast.71, bf16[8,128,576]{1,2,0:T(8,128)(2,1)S(1)} %copy-done), kind=kOutput, calls=%fused_computation.19 | convolution fusion | flops 679477248 | bytes 11943936 | tf_op jit(solution)/shard_map/dot_general | solution.py:38
  364.1 6.0 %fusion.7 = f32[4608,576]{1,0:T(8,128)} fusion(bf16[8,128,4608]{2,1,0:T(8,128)(2,1)S(1)} %bitcast.71, bf16[8,128,576]{1,2,0:T(8,128)(2,1)S(1)} %copy-done), kind=kOutput, calls=%fused_computation.21 | convolution fusion | flops 679477248 | bytes 11943936 | tf_op jit(solution)/shard_map/dot_general | solution.py:38
  370.1 37.4 %multiply_add_fusion = f32[4608,576]{1,0:T(8,128)} fusion(f32[4608,576]{1,0:T(8,128)} %fusion.1, f32[4608,576]{1,0:T(8,128)} %fusion.2, f32[4608,576]{1,0:T(8,128)} %fusion.3, f32[4608,576]{1,0:T(8,128)} %fusion.4, f32[4608,576]{1,0:T(8,128)} %fusion.5, f32[4608,576]{1,0:T(8,128)} %fusion.6, f32[4608,576]{1,0:T(8,128)} %fusion.7, f32[]{:T(128)} %bitcast.21, ...), kind=kOutput, calls=%fused_computation | convolution fusion | flops 719290368 | bytes 94523392 | tf_op jit(solution)/shard_map/dot_general | solution.py:38
  407.6 1.7 all-gather.5.cloned.1.call-done
  409.3 10.1 %fusion = bf16[72,8,8,128]{3,2,1,0:T(8,128)(2,1)S(1)} fusion(bf16[1024,4608]{1,0:T(8,128)(2,1)} %bitcast.69, bf16[576,4608]{0,1:T(8,128)(2,1)} %all-gather.5.cloned.1.call-done), kind=kOutput, calls=%fused_computation.3 | convolution fusion | flops 5436407808 | bytes 15925248 | tf_op jit(solution)/shard_map/dot_general | solution.py:19
  419.4 1.2 copy.22
  420.6 140.2 %reduce-scatter.2.cloned.1.call-done = f32[576,576]{1,0:T(8,128)} async-done(((f32[4608,576]{1,0:T(8,128)}), f32[576,576]{1,0:T(8,128)}) %reduce-scatter.2.cloned.1.call-update) | async-done | bytes 1327120 | tf_op jit(solution)/shard_map/reduce_scatter | solution.py:41
  560.8 3.0 copy.17
  (16 shorter events, 0.2 us)
Async XLA Ops:
  7.2 79.8 %all-gather.3.cloned.1.call-start = ((), (), s32[]{:S(2)}) async-start(), calls=%async_computation.2 | async-start | bytes 9732096 | tf_op jit(solution)/shard_map/all_gather | solution.py:10
  9.0 306.7 %all-reduce.2.cloned.1.call-start = ((), (), s32[]{:S(2)}) async-start(), calls=%async_computation.1 | async-start | bytes 524288 | tf_op jit(solution)/shard_map/psum | solution.py:28
  12.0 397.3 %all-gather.5.cloned.1.call-start = ((), (), s32[]{:S(2)}) async-start(), calls=%async_computation.4 | async-start | bytes 6635520 | tf_op jit(solution)/shard_map/all_gather | solution.py:21
  14.4 546.5 %reduce-scatter.2.cloned.1.call-start = ((), (), s32[]{:S(2)}) async-start(), calls=%async_computation.3 | async-start | bytes 13271040 | tf_op jit(solution)/shard_map/reduce_scatter | solution.py:41
  100.2 225.2 %copy-start = (bf16[8,128,576]{1,2,0:T(8,128)(2,1)S(1)}, bf16[8,128,576]{1,2,0:T(8,128)(2,1)}, u32[]{:S(2)}) copy-start(bf16[8,128,576]{1,2,0:T(8,128)(2,1)} %param.4) | copy-start | bytes 3538948
  324.7 8.6 %slice-start = ((s8[9437184]{0:T(1024)(128)(4,1)}), s8[4194304]{0:T(1024)(128)(4,1)S(1)}, s32[]{:S(2)}) async-start(s8[9437184]{0:T(1024)(128)(4,1)} %bitcast.70), calls=%async_computation.5 | async-start | bytes 8388608
  325.4 7.9 %slice-start.1 = ((s8[9437184]{0:T(1024)(128)(4,1)}), s8[4194304]{0:T(1024)(128)(4,1)S(1)}, s32[]{:S(2)}) async-start(s8[9437184]{0:T(1024)(128)(4,1)} %bitcast.70), calls=%async_computation.6 | async-start | bytes 8388608
  325.4 7.9 %slice-start.2 = ((s8[9437184]{0:T(1024)(128)(4,1)}), s8[1048576]{0:T(1024)(128)(4,1)S(1)}, s32[]{:S(2)}) async-start(s8[9437184]{0:T(1024)(128)(4,1)} %bitcast.70), calls=%async_computation.7 | async-start | bytes 2097152
Sparse Core Ops, SparseCore 0:
  10.4 76.4 all-gather.2
  89.5 226.0 all-reduce.1
  318.8 90.3 all-gather.4
  413.3 147.4 reduce-scatter.1
where the time goes:
time: 571 us; the launch traced here: 570 us
  waiting for transfers between devices  429 us (75%)
  matrix products  104 us (18%)
  other arithmetic  14 us (2%)
  between operations  13.8 us (2%)
  local copies, waits for them, and re-layouts  8.89 us (2%)
    psum x1, waiting for transfers between devices, body(): summed = lax.psum(hid_gram.astype(jnp.bfloat16), 'mp').astype(jnp.float32)  215 us
    reduce_scatter x1, waiting for transfers between devices, body(): local = lax.psum_scatter(running, 'dp', scatter_dimension=0, tiled=True)  140 us
    dot_general x8, matrix products, body(): lax.dot_general(part, hidden[which], (((0,), (0,)), ((), ())), preferred_...  82.1 us
    all_gather x1, waiting for transfers between devices, body(): whole = lax.all_gather(cotangent, 'mp', axis=1, tiled=True)  71.8 us
    select_n x1, other arithmetic, body(): masked = jnp.where(keep[:, :, None], whole, jnp.zeros((), whole.dtype))  13.3 us
  transfers between devices with their start and end apart: 4, of which 4 were waited for; matrix products, arithmetic and copies ran while one was open for 21% of the time, Pallas kernels for 0%

commit v1 on v0

--- a/solution.py
+++ b/solution.py
@@ -7,7 +7,10 @@
 
 def body(hidden, cotangent, w_down, lengths):
     seqs = hidden.shape[0]
-    whole = lax.all_gather(cotangent, "mp", axis=1, tiled=True)
+    n_dev = lax.axis_size("mp")
+    pieces = jnp.stack([cotangent for _ in range(n_dev)])
+    pieces = lax.all_to_all(pieces, "mp", split_axis=0, concat_axis=0)
+    whole = jnp.concatenate(pieces, axis=1)
     seq_len = whole.shape[1]
     width = whole.shape[2]
     positions = jnp.arange(seq_len, dtype=jnp.int32)

time: 571 us -> 605 us (1.060)
  local copies, waits for them, and re-layouts: 8.89 us -> 82.8 us
  waiting for transfers between devices: 429 us -> 382 us
  starting transfers between devices: 0.16 us -> 11.4 us
    all_to_all x0 -> x1, waiting for transfers between devices: none -> 206 us  [body(): pieces = lax.all_to_all(pieces, 'mp', split_axis=0, concat_axis=0)]
    psum x1, waiting for transfers between devices: 215 us -> 62.1 us  [body(): summed = lax.psum(hid_gram.astype(jnp.bfloat16), 'mp').astype(jnp.float32)]
    all_gather x1 -> x0, waiting for transfers between devices: 71.8 us -> none  [body(): whole = lax.all_gather(cotangent, 'mp', axis=1, tiled=True)]
    slice x0 -> x1, local copies, waits for them, and re-layouts: none -> 34.8 us  [body(): part = masked[which]]
    reduce_scatter x1, waiting for transfers between devices: 140 us -> 114 us  [body(): local = lax.psum_scatter(running, 'dp', scatter_dimension=0, tiled=True)]
    reshape x0 -> x2, local copies, waits for them, and re-layouts: none -> 23.4 us  [body(): whole = jnp.concatenate(pieces, axis=1)]
    all_to_all x0 -> x1, starting transfers between devices: none -> 11.3 us  [body(): pieces = lax.all_to_all(pieces, 'mp', split_axis=0, concat_axis=0)]
    all_to_all x0 -> x1, local copies, waits for them, and re-layouts: none -> 9.55 us  [body(): pieces = lax.all_to_all(pieces, 'mp', split_axis=0, concat_axis=0)]
  transfers between devices with their start and end apart: 4 -> 4, of which waited for: 4 -> 3; matrix products, arithmetic and copies ran while one was open for 21% -> 30% of each run, Pallas kernels for 0% -> 0%
where the time goes in v1:
time: 605 us; the launch traced here: 604 us
  waiting for transfers between devices  382 us (63%)
  matrix products  105 us (17%)
  local copies, waits for them, and re-layouts  82.8 us (14%)
  between operations  15.6 us (3%)
  starting transfers between devices  11.4 us (2%)
  other arithmetic  8.12 us (1%)
    all_to_all x1, waiting for transfers between devices, body(): pieces = lax.all_to_all(pieces, 'mp', split_axis=0, concat_axis=0)  206 us
    reduce_scatter x1, waiting for transfers between devices, body(): local = lax.psum_scatter(running, 'dp', scatter_dimension=0, tiled=True)  114 us
    dot_general x8, matrix products, body(): lax.dot_general(part, hidden[which], (((0,), (0,)), ((), ())), preferred_...  80.8 us
    psum x1, waiting for transfers between devices, body(): summed = lax.psum(hid_gram.astype(jnp.bfloat16), 'mp').astype(jnp.float32)  62.1 us
    slice x1, local copies, waits for them, and re-layouts, body(): part = masked[which]  34.8 us
    reshape x2, local copies, waits for them, and re-layouts, body(): whole = jnp.concatenate(pieces, axis=1)  23.4 us
  transfers between devices with their start and end apart: 4, of which 3 were waited for; matrix products, arithmetic and copies ran while one was open for 30% of the time, Pallas kernels for 0%

profile of v1, /device:TPU:1, one launch (start us, length us, event | category | flops | bytes accessed | tf_op | source)
XLA Modules:
  0.0 604.4 jit_solution(2320449250424091720)
XLA Ops:
  8.0 8.8 %stack.2 = bf16[32,8,4,4608]{3,2,1,0:T(4,128)(2,1)} broadcast(bf16[8,4,4608]{2,1,0:T(4,128)(2,1)} %param.5), dimensions={1,2,3} | broadcast | bytes 9732096 | tf_op jit(solution)/shard_map/stack | solution.py:11
  16.8 11.3 %all-to-all-start = ((bf16[32,8,4,4608]{3,2,1,0:T(4,128)(2,1)}), bf16[32,8,4,4608]{3,2,1,0:T(4,128)(2,1)}, u32[]{:S(2)}, u32[]{:S(2)}) async-start(bf16[32,8,4,4608]{3,2,1,0:T(4,128)(2,1)} %stack.2), calls=%async_computation | async-start | bytes 18874368 | tf_op jit(solution)/shard_map/all_to_all | solution.py:12
  28.2 1.3 convolution_convert_fusion
  29.6 1.2 copy.23
  31.1 206.1 %all-to-all-done = bf16[32,8,4,4608]{3,2,1,0:T(4,128)(2,1)} async-done(((bf16[32,8,4,4608]{3,2,1,0:T(4,128)(2,1)}), bf16[32,8,4,4608]{3,2,1,0:T(4,128)(2,1)}, u32[]{:S(2)}, u32[]{:S(2)}) %all-to-all-start) | async-done | bytes 9437216 | tf_op jit(solution)/shard_map/all_to_all | solution.py:12
  237.1 9.5 %copy.77 = bf16[32,8,4,4608]{3,1,2,0:T(8,128)(2,1)} copy(bf16[32,8,4,4608]{3,2,1,0:T(4,128)(2,1)} %all-to-all-done) | data formatting | bytes 18874368 | tf_op jit(solution)/shard_map/all_to_all | solution.py:12
  246.7 8.0 %bitcast_select_fusion = bf16[8,128,4608]{2,0,1:T(8,128)(2,1)} fusion(bf16[32,8,4,4608]{3,1,2,0:T(8,128)(2,1)} %copy.77, pred[8,128]{0,1:T(8,128)(4,1)S(1)} %copy.18), kind=kLoop, calls=%fused_computation.1 | loop fusion | flops 4718592 | bytes 18875392 | tf_op jit(solution)/shard_map/jit(_where)/select_n | solution.py:18
  254.7 34.8 %fusion.59 = (bf16[1,128,4608]{2,0,1:T(2,128)(2,1)}, bf16[1,128,4608]{2,0,1:T(2,128)(2,1)}, bf16[1,128,4608]{2,0,1:T(2,128)(2,1)}, bf16[1,128,4608]{2,0,1:T(2,12...) fusion(bf16[8,128,4608]{2,0,1:T(8,128)(2,1)} %bitcast_select_fusion), kind=kLoop, calls=%fused_computation.58 | loop fusion | bytes 18874368 | tf_op jit(solution)/shard_map/slice | solution.py:40
  289.5 62.1 %all-reduce.2.cloned.1.call-done = bf16[8,128,128]{2,1,0:T(8,128)(2,1)} async-done(((bf16[8,128,128]{2,1,0:T(8,128)(2,1)}), bf16[8,128,128]{2,1,0:T(8,128)(2,1)}) %all-reduce.2.cloned.1.call-update) | async-done | bytes 262160 | tf_op jit(solution)/shard_map/psum | solution.py:31
  351.6 11.8 %fusion.38 = f32[8]{0:T(128)S(1)} fusion(bf16[8,128,4608]{2,0,1:T(8,128)(2,1)} %bitcast_select_fusion, bf16[8,128,128]{2,1,0:T(8,128)(2,1)} %all-reduce.2.cloned.1.call-done), kind=kOutput, calls=%fused_computation.36 | convolution fusion | flops 1208352768 | bytes 9699360 | tf_op jit(solution)/shard_map/bsd,btd->bst/dot_general | solution.py:29
  364.1 7.9 %fusion.17 = f32[4608,576]{1,0:T(8,128)} fusion(bf16[1,128,4608]{2,0,1:T(2,128)(2,1)} %get-tuple-element.13, bf16[8,128,576]{1,2,0:T(8,128)(2,1)S(1)} %copy-done), kind=kOutput, calls=%fused_computation.15 | convolution fusion | flops 679477248 | bytes 11943936 | tf_op jit(solution)/shard_map/dot_general | solution.py:41
  372.0 6.1 %fusion.20 = f32[4608,576]{1,0:T(8,128)} fusion(bf16[1,128,4608]{2,0,1:T(2,128)(2,1)S(1)} %copy-done.5, bf16[8,128,576]{1,2,0:T(8,128)(2,1)S(1)} %copy-done), kind=kOutput, calls=%fused_computation.18 | convolution fusion | flops 679477248 | bytes 13123584 | tf_op jit(solution)/shard_map/dot_general | solution.py:41
  378.1 6.0 %fusion.23 = f32[4608,576]{1,0:T(8,128)} fusion(bf16[1,128,4608]{2,0,1:T(2,128)(2,1)S(1)} %copy-done.4, bf16[8,128,576]{1,2,0:T(8,128)(2,1)S(1)} %copy-done), kind=kOutput, calls=%fused_computation.21 | convolution fusion | flops 679477248 | bytes 13123584 | tf_op jit(solution)/shard_map/dot_general | solution.py:41
  384.1 6.2 %fusion.26 = f32[4608,576]{1,0:T(8,128)} fusion(bf16[1,128,4608]{2,0,1:T(2,128)(2,1)S(1)} %copy-done.3, bf16[8,128,576]{1,2,0:T(8,128)(2,1)S(1)} %copy-done), kind=kOutput, calls=%fused_computation.24 | convolution fusion | flops 679477248 | bytes 13123584 | tf_op jit(solution)/shard_map/dot_general | solution.py:41
  390.4 6.1 %fusion.29 = f32[4608,576]{1,0:T(8,128)} fusion(bf16[1,128,4608]{2,0,1:T(2,128)(2,1)S(1)} %copy-done.2, bf16[8,128,576]{1,2,0:T(8,128)(2,1)S(1)} %copy-done), kind=kOutput, calls=%fused_computation.27 | convolution fusion | flops 679477248 | bytes 13123584 | tf_op jit(solution)/shard_map/dot_general | solution.py:41
  396.5 6.0 fusion.32
  402.5 6.0 fusion.35
  408.5 36.5 %multiply_add_fusion = f32[4608,576]{1,0:T(8,128)} fusion(f32[4608,576]{1,0:T(8,128)} %fusion.17, f32[4608,576]{1,0:T(8,128)} %fusion.20, f32[4608,576]{1,0:T(8,128)} %fusion.23, f32[4608,576]{1,0:T(8,128)} %fusion.26, f32[4608,576]{1,0:T(8,128)} %fusion.29, f32[4608,576]{1,0:T(8,128)} %fusion.32, f32[4608,576]{1,0:T(8,128)} %fusion.35, f32[]{:T(128)} %bitcast.16, ...), kind=kOutput, calls=%fused_computation | convolution fusion | flops 719290368 | bytes 87441440 | tf_op jit(solution)/shard_map/dot_general | solution.py:41
  444.9 10.3 %copy.22 = bf16[8,32,4,4608]{3,2,1,0:T(4,128)(2,1)} copy(bf16[8,32,4,4608]{3,0,2,1:T(8,128)(2,1)} %bitcast.73) | data formatting | bytes 18874368 | tf_op jit(solution)/shard_map/reshape | solution.py:13
  455.3 13.1 %reshape.47 = bf16[1024,4608]{1,0:T(8,128)(2,1)} reshape(bf16[8,32,4,4608]{3,2,1,0:T(4,128)(2,1)} %copy.22) | data formatting | bytes 18874368 | tf_op jit(solution)/shard_map/reshape | solution.py:13
  468.4 10.7 %fusion.9 = bf16[72,8,8,128]{3,2,1,0:T(8,128)(2,1)S(1)} fusion(bf16[576,4608]{0,1:T(8,128)(2,1)} %all-gather.2.cloned.1.call-done, bf16[1024,4608]{1,0:T(8,128)(2,1)} %reshape.47, pred[1024]{0:T(1024)(128)(4,1)S(1)} %get-tuple-element.20), kind=kOutput, calls=%fused_computation.9 | convolution fusion | flops 5441126400 | bytes 15926272 | tf_op jit(solution)/shard_map/dot_general | solution.py:22
  479.1 1.2 copy.76
  480.3 113.7 %reduce-scatter.2.cloned.1.call-done = f32[576,576]{1,0:T(8,128)} async-done(((f32[4608,576]{1,0:T(8,128)}), f32[576,576]{1,0:T(8,128)}) %reduce-scatter.2.cloned.1.call-update) | async-done | bytes 1327120 | tf_op jit(solution)/shard_map/reduce_scatter | solution.py:44
  594.0 3.0 copy.24
  (29 shorter events, 1.1 us)
Async XLA Ops:
  16.8 11.4 %copy-start = (bf16[8,128,576]{1,2,0:T(8,128)(2,1)S(1)}, bf16[8,128,576]{1,2,0:T(8,128)(2,1)}, u32[]{:S(2)}) copy-start(bf16[8,128,576]{1,2,0:T(8,128)(2,1)} %param.4) | copy-start | bytes 3538948
  16.8 220.3 %all-to-all-start = ((bf16[32,8,4,4608]{3,2,1,0:T(4,128)(2,1)}), bf16[32,8,4,4608]{3,2,1,0:T(4,128)(2,1)}, u32[]{:S(2)}, u32[]{:S(2)}) async-start(bf16[32,8,4,4608]{3,2,1,0:T(4,128)(2,1)} %stack.2), calls=%async_computation | async-start | bytes 18874368 | tf_op jit(solution)/shard_map/all_to_all | solution.py:12
  28.2 1.4 copy-start.7
  28.2 2.7 copy-start.8
  28.2 323.4 %all-reduce.2.cloned.1.call-start = ((), (), s32[]{:S(2)}) async-start(), calls=%async_computation.2 | async-start | bytes 524288 | tf_op jit(solution)/shard_map/psum | solution.py:31
  29.6 438.8 %all-gather.2.cloned.1.call-start = ((), (), s32[]{:S(2)}) async-start(), calls=%async_computation.4 | async-start | bytes 6635520 | tf_op jit(solution)/shard_map/all_gather | solution.py:24
  30.8 563.2 %reduce-scatter.2.cloned.1.call-start = ((), (), s32[]{:S(2)}) async-start(), calls=%async_computation.3 | async-start | bytes 13271040 | tf_op jit(solution)/shard_map/reduce_scatter | solution.py:44
  364.0 7.9 %copy-start.5 = (bf16[1,128,4608]{2,0,1:T(2,128)(2,1)S(1)}, bf16[1,128,4608]{2,0,1:T(2,128)(2,1)}, u32[]{:S(2)}) copy-start(bf16[1,128,4608]{2,0,1:T(2,128)(2,1)} %get-tuple-element.14) | copy-start | bytes 3538948
  372.0 6.1 %copy-start.4 = (bf16[1,128,4608]{2,0,1:T(2,128)(2,1)S(1)}, bf16[1,128,4608]{2,0,1:T(2,128)(2,1)}, u32[]{:S(2)}) copy-start(bf16[1,128,4608]{2,0,1:T(2,128)(2,1)} %get-tuple-element.15) | copy-start | bytes 3538948
  378.1 6.1 %copy-start.3 = (bf16[1,128,4608]{2,0,1:T(2,128)(2,1)S(1)}, bf16[1,128,4608]{2,0,1:T(2,128)(2,1)}, u32[]{:S(2)}) copy-start(bf16[1,128,4608]{2,0,1:T(2,128)(2,1)} %get-tuple-element.16) | copy-start | bytes 3538948
  384.1 6.2 %copy-start.2 = (bf16[1,128,4608]{2,0,1:T(2,128)(2,1)S(1)}, bf16[1,128,4608]{2,0,1:T(2,128)(2,1)}, u32[]{:S(2)}) copy-start(bf16[1,128,4608]{2,0,1:T(2,128)(2,1)} %get-tuple-element.17) | copy-start | bytes 3538948
  390.4 6.1 %copy-start.1 = (bf16[1,128,4608]{2,0,1:T(2,128)(2,1)S(1)}, bf16[1,128,4608]{2,0,1:T(2,128)(2,1)}, u32[]{:S(2)}) copy-start(bf16[1,128,4608]{2,0,1:T(2,128)(2,1)} %get-tuple-element.18) | copy-start | bytes 3538948
  402.5 6.0 copy-start.6
Sparse Core Ops, SparseCore 0:
  32.2 319.3 all-reduce.1
Sparse Core Ops, SparseCore 1:
  33.2 129.5 all-gather.1
  445.0 148.9 reduce-scatter.1
